TPU v7x, 512 devices: a whole 4x4x16 slice. The times are simulated.
512 devices in a mesh: col: 64 (over y, x, z_lo), row: 8 (over z_hi, core).
Axes of the slice: x: 4, y: 4, z: 16 (z_hi: 4, z_lo: 4; z = z_hi * 4 + z_lo), core: 2. Of those that a mesh axis runs over, the one named last changes fastest.
Arguments:
- slab_embed: float32 [64, 4096], P(None, 'row'), may hold values from -6 to 6
- slab_probe: float32 [32, 4096], P(None, 'row'), may hold values from -6 to 6
- point_embed: float32 [64, 131072], P(None, 'col'), may hold values from -6 to 6
- point_probe: float32 [32, 131072], P(None, 'col'), may hold values from -1.2 to 1.2
- inv_scale: float32 [64], replicated, may hold values from 0.08 to 0.3
Outputs:
- slab_grad: float32 [64, 4096], P(None, 'row')
- point_grad: float32 [64, 131072], P(None, 'col')
All inputs are finite; a program needn't handle non-finite values.
Results may differ from a plain program's by a relative error of at most 0.0001.
Values sent between devices are 32-bit elements; how exact they have to be, the bound alone decides.
A program may use at most 64 MiB of HBM per device.

v0:
```python
import jax
import jax.numpy as jnp
from jax import lax
from jax.sharding import PartitionSpec as P


def local(slab_embed, slab_probe, point_embed, point_probe, inv_scale):
    hp = lax.Precision.HIGHEST
    weight_sq = inv_scale * inv_scale
    scaled = slab_embed * weight_sq[:, None]
    self_term = jnp.sum(scaled * slab_embed, axis=0)
    points_here = point_embed.shape[1]
    width = min(1024, points_here)
    row_total = jnp.zeros((slab_embed.shape[1],), jnp.float32)
    mixed = jnp.zeros(slab_embed.shape, jnp.float32)
    pieces = []
    for block in range(points_here // width):
        points = point_embed[:, block * width : (block + 1) * width]
        probes = point_probe[:, block * width : (block + 1) * width]
        other_term = jnp.sum(weight_sq[:, None] * points * points, axis=0)
        cross = jnp.dot(scaled.T, points, precision=hp)
        kernel = jnp.exp(-0.5 * (self_term[:, None] + other_term[None, :] - 2.0 * cross))
        weights = kernel * jnp.dot(slab_probe.T, probes, precision=hp)
        row_total = row_total + jnp.sum(weights, axis=1)
        mixed = mixed + jnp.dot(points, weights.T, precision=hp)
        pieces.append(
            weight_sq[:, None]
            * (
                jnp.dot(slab_embed, weights, precision=hp)
                - points * jnp.sum(weights, axis=0)[None, :]
            )
        )
    slab_terms = -weight_sq[:, None] * (slab_embed * row_total[None, :] - mixed)
    point_terms = jnp.concatenate(pieces, axis=1)
    slab_grad = lax.psum(slab_terms, "col")
    point_grad = lax.psum(point_terms, "row")
    return (slab_grad, point_grad)


def solution(mesh):
    placed = (P(None, "row"), P(None, "row"), P(None, "col"), P(None, "col"), P())
    return jax.shard_map(
        local,
        mesh=mesh,
        in_specs=placed,
        out_specs=(P(None, "row"), P(None, "col")),
        check_vma=False,
    )
```

profile of v0, /device:TPU:1, one launch (start us, length us, event | category | flops | bytes accessed | tf_op | source)
XLA Modules:
  0.0 783.1 jit_solution(10574615676581666491)
XLA Ops:
  7.2 0.0 copy-start
  7.2 0.0 copy-start.4
  7.2 0.0 copy-start.3
  7.2 0.0 all-reduce.3.cloned.1.call-start
  7.2 0.7 multiply_negate_fusion
  8.0 1.0 fusion.18
  9.0 1.2 fusion.8
  10.2 0.0 copy-start.5
  10.2 3.0 fusion.14
  13.2 0.0 copy-done.4
  13.2 0.0 copy-done.3
  13.2 1.9 fusion.10
  15.1 0.0 copy-done
  15.1 0.0 copy-done.5
  15.1 2.4 fusion.23
  17.5 2.2 fusion.12
  19.6 2.4 fusion.24
  22.0 0.0 copy-start.1
  22.1 1.3 copy-done.1
  23.4 2.8 fusion.6
  26.2 0.0 all-reduce.3.cloned.1.call-update
  26.2 0.2 all-reduce.5.cloned.1.call-start
  26.5 0.0 copy-start.2
  26.5 1.5 fusion.3
  27.9 0.1 copy-done.2
  28.1 1.5 fusion.1
  29.5 0.8 pad_maximum_fusion
  30.3 0.0 all-reduce.5.cloned.1.call-update
  30.4 622.6 %all-reduce.3.cloned.1.call-done = f32[64,512]{1,0:T(8,128)} async-done(((f32[64,512]{1,0:T(8,128)}), f32[64,512]{1,0:T(8,128)}) %all-reduce.3.cloned.1.call-update) | async-done | bytes 131088 | tf_op jit(solution)/shard_map/psum | solution.py:35
  652.9 119.9 %all-reduce.5.cloned.1.call-done = f32[64,2048]{1,0:T(8,128)} async-done(((f32[64,2048]{1,0:T(8,128)}), f32[64,2048]{1,0:T(8,128)}) %all-reduce.5.cloned.1.call-update) | async-done | bytes 524304 | tf_op jit(solution)/shard_map/psum | solution.py:36
  772.8 1.6 copy.9
  774.4 1.9 copy.10
  (1 shorter events, 0.0 us)
Async XLA Ops:
  7.2 7.9 %copy-start = (f32[32,512]{1,0:T(8,128)S(1)}, f32[32,512]{1,0:T(8,128)}, u32[]{:S(2)}) copy-start(f32[32,512]{1,0:T(8,128)} %param.6) | copy-start | bytes 196612
  7.2 6.0 copy-start.4
  7.2 6.0 copy-start.3
  7.2 645.7 %all-reduce.3.cloned.1.call-start = ((), (), s32[]{:S(2)}) async-start(), calls=%async_computation | async-start | bytes 262144 | tf_op jit(solution)/shard_map/psum | solution.py:35
  10.2 4.9 copy-start.5
  22.0 1.4 copy-start.1
  26.2 746.6 %all-reduce.5.cloned.1.call-start = ((), (), s32[]{:S(2)}) async-start(), calls=%async_computation.1 | async-start | bytes 1048576 | tf_op jit(solution)/shard_map/psum | solution.py:36
  26.5 1.6 copy-start.2
Sparse Core Ops, SparseCore 0:
  26.4 626.5 all-reduce.2
  656.7 116.1 all-reduce.4
where the time goes:
time: 783 us
  waiting for transfers between devices  743 us (95%)
  matrix products  17.5 us (2%)
  between operations  14.1 us (2%)
    psum x1, waiting for transfers between devices, local(): slab_grad = lax.psum(slab_terms, 'col')  623 us
    psum x1, waiting for transfers between devices, local(): point_grad = lax.psum(point_terms, 'row')  120 us
  transfers between devices with their start and end apart: 2, of which 2 were waited for; matrix products, arithmetic and copies ran while one was open for 0% of the time, Pallas kernels for 0%

commit v1 on v0

v1 whole, which is shorter than its diff:
```python
import math

import jax
import jax.numpy as jnp
from jax import lax
from jax.experimental import pallas as pl
from jax.experimental.pallas import tpu as pltpu
from jax.sharding import PartitionSpec as P

MESH = pl.DeviceIdType.MESH
F32 = jnp.float32
BF16 = jnp.bfloat16
LOG2E = math.log2(math.e)
EMB = 64
PROBES = 32
ROWS = 512
PIECE = 512
UNIT = 256
HALF = 32


def split3(v):
    high = v.astype(BF16)
    rest = v - high.astype(F32)
    mid = rest.astype(BF16)
    low = (rest - mid.astype(F32)).astype(BF16)
    return high, mid, low


def matmul(a, b, contract):
    return lax.dot_general(a, b, ((contract[:1], contract[1:]), ((), ())), preferred_element_type=F32)


def kernel(
    scale_ref,
    slab_ref,
    slab_probe_ref,
    point_ref,
    point_probe_ref,
    slab_out,
    point_out,
    left_c,
    left_p,
    left_s,
    part,
    sib_in,
    r1,
    r2,
    full,
    sp,
    sx_in,
    sx,
    sy_in,
    sz,
    sf,
    send,
    recv,
):
    row, col = lax.axis_index("row"), lax.axis_index("col")
    core, q = lax.rem(row, 2), row // 2
    zl, x, y = lax.rem(col, 4), lax.rem(col // 4, 4), col // 16
    other = 1 - core

    def at_z(k):
        return (col, lax.rem(q + k, 4) * 2 + core)

    sibling = (col, q * 2 + other)
    z_up, z_down = at_z(1), at_z(3)

    def at_x(k):
        return (y * 16 + lax.rem(x + k, 4) * 4 + zl, row)

    def at_y(k):
        return (lax.rem(y + k, 4) * 16 + x * 4 + zl, row)

    def at_l(k):
        return (y * 16 + x * 4 + lax.rem(zl + k, 4), row)

    partners = [sibling, z_up, z_down]
    for k in (1, 2, 3):
        partners += [at_x(k), at_y(k), at_l(k)]
    barrier = pltpu.get_barrier_semaphore()
    for device in partners:
        pl.semaphore_signal(barrier, inc=1, device_id=device, device_id_type=MESH)

    count = [0]

    def copy(src, dst, device):
        i = count[0]
        count[0] += 1
        return pltpu.make_async_remote_copy(
            src_ref=src, dst_ref=dst, send_sem=send.at[i], recv_sem=recv.at[i],
            device_id=device, device_id_type=MESH,
        )

    diag = lax.broadcasted_iota(jnp.int32, (EMB, EMB), 0) == lax.broadcasted_iota(jnp.int32, (EMB, EMB), 1)
    scale = jnp.sum(jnp.where(diag, scale_ref[...], 0.0), axis=1, keepdims=True)
    w2 = scale * scale
    slab = slab_ref[...]
    scaled = slab * w2
    self_term = jnp.sum(scaled * slab, axis=0, keepdims=True) * (-0.5 * LOG2E)
    xh, xm, xl = split3(scaled * LOG2E)
    lane_id = lax.broadcasted_iota(jnp.int32, (16, ROWS), 0)

    def extras(term, first):
        th, tm, tl = (t.astype(F32) for t in split3(term))
        base = jnp.where(lane_id < 6, 1.0, 0.0)
        base = jnp.where(lane_id == first, th, base)
        base = jnp.where(lane_id == first + 1, tm, base)
        base = jnp.where(lane_id == first + 2, tl, base)
        return base.astype(BF16)

    left_c[...] = jnp.concatenate([xh, xh, xm, xh, xl, xm, extras(self_term, 0)], axis=0).T
    ph, pm, pl_ = split3(slab_probe_ref[...])
    left_p[...] = jnp.concatenate([ph, ph, pm, ph, pl_, pm], axis=0).T
    sh, sm, sl = split3(slab)
    ones = jnp.ones((16, ROWS), BF16)
    left_s[...] = jnp.concatenate([sh, sm, sl, ones], axis=0)

    def compute(j, piece, total):
        for u in range(2):
            cols = pl.ds(pl.multiple_of(piece * PIECE + u * UNIT, UNIT), UNIT)
            points = point_ref[:, cols]
            probes = point_probe_ref[:, cols]
            other_term = jnp.sum(w2 * points * points, axis=0, keepdims=True) * (-0.5 * LOG2E)
            yh, ym, yl = split3(points)
            th, tm, tl = (t.astype(F32) for t in split3(other_term))
            ids = lane_id[:, :UNIT]
            base = jnp.where(ids < 6, 1.0, 0.0)
            base = jnp.where(ids == 3, th, base)
            base = jnp.where(ids == 4, tm, base)
            base = jnp.where(ids == 5, tl, base)
            right_c = jnp.concatenate([yh, ym, yh, yl, yh, ym, base.astype(BF16)], axis=0)
            gh, gm, gl = split3(probes)
            right_p = jnp.concatenate([gh, gm, gh, gl, gh, gm], axis=0)
            exponent = matmul(left_c[...], right_c, (1, 0))
            weights = jnp.exp2(exponent) * matmul(left_p[...], right_p, (1, 0))
            mh = weights.astype(BF16)
            ml = (weights - mh.astype(F32)).astype(BF16)
            ls = left_s[...]
            o2 = matmul(ls, mh, (1, 0)) + matmul(ls, ml, (1, 0))
            right_s = jnp.concatenate([yh, ym, yl, ones[:, :UNIT]], axis=0)
            o1 = matmul(right_s, mh, (1, 1)) + matmul(right_s, ml, (1, 1))
            total = o1 if total is None else total + o1
            mixed = o2[0:64] + o2[64:128] + o2[128:192]
            terms = w2 * (mixed - points * o2[192:193])
            part[j, 0, u] = terms[:HALF]
            part[j, 1, u] = terms[HALF:]
        return total

    def to_sibling(j):
        c = copy(part.at[j, other], sib_in.at[j], sibling)
        c.start()
        return c

    def take_sibling(j, c):
        c.wait_recv()
        part[j, core] = part[j, core] + sib_in[j]

    done = []

    def go(src, dst, device):
        c = copy(src, dst, device)
        c.start()
        done.append(c)
        return c

    p_up, p_down, p_far = lax.rem(q + 1, 4), lax.rem(q + 3, 4), lax.rem(q + 2, 4)

    total = compute(0, p_far, None)
    pl.semaphore_wait(barrier, len(partners))
    s0 = to_sibling(0)
    total = compute(1, p_up, total)
    take_sibling(0, s0)
    a0 = go(part.at[0, core, 0], r1.at[0], z_down)
    a1 = go(part.at[0, core, 1], r1.at[1], z_up)
    s1 = to_sibling(1)
    total = compute(2, p_down, total)
    take_sibling(1, s1)
    b1 = go(part.at[1, core, 0], r2.at[1, 0], z_up)
    s2 = to_sibling(2)
    total = compute(3, q, total)
    take_sibling(2, s2)
    b0 = go(part.at[2, core, 1], r2.at[0, 1], z_down)
    s3 = to_sibling(3)

    slab_mixed = total[0:64] + total[64:128] + total[128:192]
    slab_terms = w2 * (slab_mixed - slab * total[192:193])
    for i in range(4):
        for k in range(4):
            sp[i, k] = slab_terms[16 * i : 16 * i + 16, 128 * k : 128 * k + 128]
    cx = [go(sp.at[lax.rem(x + k, 4)], sx_in.at[k - 1], at_x(k)) for k in (1, 2, 3)]

    take_sibling(3, s3)
    a0.wait_recv()
    part[2, core, 0] = part[2, core, 0] + r1[0]
    b2 = go(part.at[2, core, 0], r2.at[0, 0], z_down)
    a1.wait_recv()
    part[1, core, 1] = part[1, core, 1] + r1[1]
    b3 = go(part.at[1, core, 1], r2.at[1, 1], z_up)

    for c in cx:
        c.wait_recv()
    sx[...] = sp[x] + sx_in[0] + sx_in[1] + sx_in[2]
    cy = [go(sx.at[lax.rem(y + k, 4)], sy_in.at[k - 1], at_y(k)) for k in (1, 2, 3)]
    for c in cy:
        c.wait_recv()
    sz[zl] = sx[y] + sy_in[0] + sy_in[1] + sy_in[2]
    cl = [go(sz.at[zl], sz.at[zl], at_l(k)) for k in (1, 2, 3)]

    b0.wait_recv()
    b1.wait_recv()
    b2.wait_recv()
    full[q, core, 0] = part[3, core, 0] + r2[0, 0] + r2[1, 0]
    d0 = go(full.at[q, core, 0], full.at[q, core, 0], z_down)
    b3.wait_recv()
    full[q, core, 1] = part[3, core, 1] + r2[0, 1] + r2[1, 1]
    d1 = go(full.at[q, core, 1], full.at[q, core, 1], z_up)
    d2 = go(full.at[q, core, 0], full.at[q, core, 0], z_up)
    d3 = go(full.at[q, core, 1], full.at[q, core, 1], z_down)
    e = [go(full.at[q, core], full.at[q, core], sibling)]

    for c in cl:
        c.wait_recv()
    sf[x, y] = sz[0] + sz[1] + sz[2] + sz[3]
    cy = [go(sf.at[x, y], sf.at[x, y], at_y(k)) for k in (1, 2, 3)]

    d0.wait_recv()
    f0 = go(full.at[p_up, core, 0], full.at[p_up, core, 0], z_down)
    d1.wait_recv()
    f1 = go(full.at[p_down, core, 1], full.at[p_down, core, 1], z_up)
    for c in cy:
        c.wait_recv()
    cx = [go(sf.at[x], sf.at[x], at_x(k)) for k in (1, 2, 3)]
    d2.wait_recv()
    e.append(go(full.at[p_down, core], full.at[p_down, core], sibling))
    d3.wait_recv()
    e.append(go(full.at[p_up, core], full.at[p_up, core], sibling))
    f0.wait_recv()
    e.append(go(full.at[p_far, core, 0], full.at[p_far, core, 0], sibling))
    f1.wait_recv()
    e.append(go(full.at[p_far, core, 1], full.at[p_far, core, 1], sibling))

    for c in cx:
        c.wait_recv()
    for i in range(4):
        for k in range(4):
            slab_out[16 * i : 16 * i + 16, 128 * k : 128 * k + 128] = sf[i, k]
    for c in e:
        c.wait_recv()
    for o in range(4):
        for h in range(2):
            for u in range(2):
                lo = o * PIECE + u * UNIT
                point_out[h * HALF : h * HALF + HALF, lo : lo + UNIT] = full[o, h, u]
    for c in [s0, s1, s2, s3] + done:
        c.wait_send()


def local(slab_embed, slab_probe, point_embed, point_probe, inv_scale):
    vmem = pl.BlockSpec(memory_space=pltpu.VMEM)
    return pl.pallas_call(
        kernel,
        name="pathwise_grad",
        out_shape=(
            jax.ShapeDtypeStruct(slab_embed.shape, F32),
            jax.ShapeDtypeStruct(point_embed.shape, F32),
        ),
        in_specs=[vmem] * 5,
        out_specs=(vmem, vmem),
        scratch_shapes=[
            pltpu.VMEM((ROWS, 6 * EMB + 16), BF16),
            pltpu.VMEM((ROWS, 6 * PROBES), BF16),
            pltpu.VMEM((3 * EMB + 16, ROWS), BF16),
            pltpu.VMEM((4, 2, 2, HALF, UNIT), F32),
            pltpu.VMEM((4, 2, HALF, UNIT), F32),
            pltpu.VMEM((2, HALF, UNIT), F32),
            pltpu.VMEM((2, 2, HALF, UNIT), F32),
            pltpu.VMEM((4, 2, 2, HALF, UNIT), F32),
            pltpu.VMEM((4, 4, 16, 128), F32),
            pltpu.VMEM((3, 4, 16, 128), F32),
            pltpu.VMEM((4, 16, 128), F32),
            pltpu.VMEM((3, 16, 128), F32),
            pltpu.VMEM((4, 16, 128), F32),
            pltpu.VMEM((4, 4, 16, 128), F32),
            pltpu.SemaphoreType.DMA((40,)),
            pltpu.SemaphoreType.DMA((40,)),
        ],
        compiler_params=pltpu.CompilerParams(
            collective_id=0, has_side_effects=True, vmem_limit_bytes=40 * 1024 * 1024
        ),
    )(inv_scale.reshape(1, EMB), slab_embed, slab_probe, point_embed, point_probe)


def solution(mesh):
    placed = (P(None, "row"), P(None, "row"), P(None, "col"), P(None, "col"), P())
    return jax.shard_map(
        local,
        mesh=mesh,
        in_specs=placed,
        out_specs=(P(None, "row"), P(None, "col")),
        check_vma=False,
    )
```

time: 783 us -> 47.8 us (0.06)
  waiting for transfers between devices: 743 us -> 0 us
  Pallas kernels: 0 us -> 40.9 us
  matrix products: 17.5 us -> 0 us
  between operations: 14.1 us -> 0.65 us
    psum x2 -> x0, waiting for transfers between devices: 742 us -> none  [the longest x1 623 us: local(): slab_grad = lax.psum(slab_terms, 'col')]
    pallas_call x0 -> x1, Pallas kernels: none -> 40.9 us  [local(): pl.pallas_call(kernel, name='pathwise_grad', out_shape=(jax.ShapeDtypeStr...]
    dot_general x8 -> x0, matrix products: 17.5 us -> none  [the longest x2 4.97 us: local(): mixed = mixed + jnp.dot(points, weights.T, precision=hp)]
  transfers between devices with their start and end apart: 2 -> 0, of which waited for: 2 -> 0; matrix products, arithmetic and copies ran while one was open for 0% -> 0% of each run, Pallas kernels for 0% -> 0%
where the time goes in v1:
time: 47.8 us; the launch traced here: 47.4 us
  Pallas kernels  40.9 us (86%)
  local copies, waits for them, and re-layouts  5.83 us (12%)
  between operations  0.65 us (1%)
    pallas_call x1, Pallas kernels, local(): pl.pallas_call(kernel, name='pathwise_grad', out_shape=(jax.ShapeDtypeStr...  40.9 us
    unnamed x12, local copies, waits for them, and re-layouts  5.83 us

profile of v1, /device:TPU:1, one launch (start us, length us, event | category | flops | bytes accessed | tf_op | source)
XLA Modules:
  0.0 47.4 jit_solution(15301295339813015365)
XLA Ops:
  0.6 0.0 copy-start.4
  0.6 0.6 %copy-done.4 = f32[64]{0:T(128)S(1)} copy-done((f32[64]{0:T(128)S(1)}, f32[64]{0:T(128)}, u32[]{:S(2)}) %copy-start.4) | copy-done | bytes 280
  1.3 0.0 copy-start
  1.3 1.0 %copy-done = f32[64,2048]{1,0:T(8,128)S(1)} copy-done((f32[64,2048]{1,0:T(8,128)S(1)}, f32[64,2048]{1,0:T(8,128)}, u32[]{:S(2)}) %copy-start) | copy-done | bytes 524312
  2.3 0.0 copy-start.1
  2.3 0.9 %copy-done.1 = f32[32,2048]{1,0:T(8,128)S(1)} copy-done((f32[32,2048]{1,0:T(8,128)S(1)}, f32[32,2048]{1,0:T(8,128)}, u32[]{:S(2)}) %copy-start.1) | copy-done | bytes 262168
  3.3 0.0 copy-start.2
  3.3 0.9 %copy-done.2 = f32[64,512]{1,0:T(8,128)S(1)} copy-done((f32[64,512]{1,0:T(8,128)S(1)}, f32[64,512]{1,0:T(8,128)}, u32[]{:S(2)}) %copy-start.2) | copy-done | bytes 131096
  4.2 0.0 copy-start.3
  4.2 0.8 %copy-done.3 = f32[32,512]{1,0:T(8,128)S(1)} copy-done((f32[32,512]{1,0:T(8,128)S(1)}, f32[32,512]{1,0:T(8,128)}, u32[]{:S(2)}) %copy-start.3) | copy-done | bytes 65560
  5.0 40.9 %pathwise_grad.1 = (f32[64,512]{1,0:T(8,128)S(1)}, f32[64,2048]{1,0:T(8,128)S(1)}) custom-call(f32[1,64]{1,0:T(1,128)S(1)} %bitcast.1, f32[64,512]{1,0:T(8,128)S(1)} %copy-done.2, f32[32,512]{1,0:T(8,128)S(1)} %copy-done.3, f32[64,2048]{1,0:T(8,128)S(1)} %copy-done, f32[32,2048]{1,0:T(8,128)S(1)} %copy-done.1), custom_call_target="tpu_custom_call" | custom-call | tf_op jit(solution)/shard_map/pathwise_grad/pallas_call | solution.py:262
  45.9 0.7 %copy.9 = f32[64,512]{1,0:T(8,128)} copy(f32[64,512]{1,0:T(8,128)S(1)} %get-tuple-element.4) | data formatting | bytes 262144
  46.6 0.8 %copy.10 = f32[64,2048]{1,0:T(8,128)} copy(f32[64,2048]{1,0:T(8,128)S(1)} %get-tuple-element.5) | data formatting | bytes 1048576
Async XLA Ops:
  0.6 0.7 %copy-start.4 = (f32[64]{0:T(128)S(1)}, f32[64]{0:T(128)}, u32[]{:S(2)}) copy-start(f32[64]{0:T(128)} %param.9) | copy-start | bytes 772
  1.3 1.0 %copy-start = (f32[64,2048]{1,0:T(8,128)S(1)}, f32[64,2048]{1,0:T(8,128)}, u32[]{:S(2)}) copy-start(f32[64,2048]{1,0:T(8,128)} %point_ref.1) | copy-start | bytes 1572868
  2.3 0.9 %copy-start.1 = (f32[32,2048]{1,0:T(8,128)S(1)}, f32[32,2048]{1,0:T(8,128)}, u32[]{:S(2)}) copy-start(f32[32,2048]{1,0:T(8,128)} %point_probe_ref.1) | copy-start | bytes 786436
  3.3 0.9 %copy-start.2 = (f32[64,512]{1,0:T(8,128)S(1)}, f32[64,512]{1,0:T(8,128)}, u32[]{:S(2)}) copy-start(f32[64,512]{1,0:T(8,128)} %slab_ref.1) | copy-start | bytes 393220
  4.2 0.8 %copy-start.3 = (f32[32,512]{1,0:T(8,128)S(1)}, f32[32,512]{1,0:T(8,128)}, u32[]{:S(2)}) copy-start(f32[32,512]{1,0:T(8,128)} %slab_probe_ref.1) | copy-start | bytes 196612

commit v2 on v0

v2 whole, which is shorter than its diff:
```python
import math

import jax
import jax.numpy as jnp
from jax import lax
from jax.experimental import pallas as pl
from jax.experimental.pallas import tpu as pltpu
from jax.sharding import PartitionSpec as P

MESH = pl.DeviceIdType.MESH
F32 = jnp.float32
BF16 = jnp.bfloat16
LOG2E = math.log2(math.e)
EMB = 64
PROBES = 32
ROWS = 512
PIECE = 512
UNIT = 256
VMEM_MIB = 40
HALF = 32


def split3(v):
    high = v.astype(BF16)
    rest = v - high.astype(F32)
    mid = rest.astype(BF16)
    low = (rest - mid.astype(F32)).astype(BF16)
    return high, mid, low


def matmul(a, b, contract):
    return lax.dot_general(a, b, ((contract[:1], contract[1:]), ((), ())), preferred_element_type=F32)


def kernel(
    scale_hbm,
    slab_hbm,
    slab_probe_hbm,
    point_hbm,
    point_probe_hbm,
    slab_out,
    point_out,
    scale_ref,
    slab_ref,
    slab_probe_ref,
    point_ref,
    point_probe_ref,
    left_c,
    left_p,
    left_s,
    part,
    sib_in,
    r1,
    r2,
    full,
    sp,
    sx_in,
    sx,
    sy_in,
    sz,
    sf,
    load,
    send,
    recv,
):
    row, col = lax.axis_index("row"), lax.axis_index("col")
    core, q = lax.rem(row, 2), row // 2
    zl, x, y = lax.rem(col, 4), lax.rem(col // 4, 4), col // 16
    other = 1 - core
    p_up, p_down, p_far = lax.rem(q + 1, 4), lax.rem(q + 3, 4), lax.rem(q + 2, 4)
    pieces = (p_far, p_up, p_down, q)

    def columns(j, u):
        return pl.ds(pl.multiple_of(pieces[j] * PIECE + u * UNIT, UNIT), UNIT)

    loads = [
        pltpu.make_async_copy(scale_hbm, scale_ref, load.at[0]),
        pltpu.make_async_copy(slab_hbm, slab_ref, load.at[1]),
        pltpu.make_async_copy(slab_probe_hbm, slab_probe_ref, load.at[2]),
        pltpu.make_async_copy(point_hbm, point_ref, load.at[3]),
        pltpu.make_async_copy(point_probe_hbm, point_probe_ref, load.at[4]),
    ]
    for c in loads:
        c.start()

    def at_z(k):
        return (col, lax.rem(q + k, 4) * 2 + core)

    sibling = (col, q * 2 + other)
    z_up, z_down = at_z(1), at_z(3)

    def in_plane(i, k):
        return (lax.rem(y + k, 4) * 16 + lax.rem(x + i, 4) * 4 + zl, row)

    def at_l(k):
        return (y * 16 + x * 4 + lax.rem(zl + k, 4), row)

    partners = [sibling, z_up, z_down]
    for k in (1, 2, 3):
        partners += [in_plane(k, 0), in_plane(0, k), at_l(k)]
    barrier = pltpu.get_barrier_semaphore()
    for device in partners:
        pl.semaphore_signal(barrier, inc=1, device_id=device, device_id_type=MESH)

    sent = []

    def go(src, dst, device):
        i = len(sent)
        c = pltpu.make_async_remote_copy(
            src_ref=src, dst_ref=dst, send_sem=send.at[i], recv_sem=recv.at[i],
            device_id=device, device_id_type=MESH,
        )
        c.start()
        sent.append(c)
        return c

    diag = lax.broadcasted_iota(jnp.int32, (EMB, EMB), 0) == lax.broadcasted_iota(jnp.int32, (EMB, EMB), 1)
    row_id = lax.broadcasted_iota(jnp.int32, (16, ROWS), 0)
    ones = jnp.ones((16, ROWS), BF16)

    def extras(term, first, width):
        ids = row_id[:, :width]
        base = jnp.where(ids < 6, 1.0, 0.0)
        for i, t in enumerate(split3(term)):
            base = jnp.where(ids == first + i, t.astype(F32), base)
        return base.astype(BF16)

    loads[0].wait()
    loads[1].wait()
    scale = jnp.sum(jnp.where(diag, scale_ref[...], 0.0), axis=1, keepdims=True)
    w2 = scale * scale
    slab = slab_ref[...]
    scaled = slab * w2
    self_term = jnp.sum(scaled * slab, axis=0, keepdims=True) * (-0.5 * LOG2E)
    xh, xm, xl = split3(scaled * LOG2E)
    hm = jnp.concatenate([xh, xm], axis=0).T
    left_c[:, 0:128] = hm
    left_c[:, 128:256] = hm
    left_c[:, 256:384] = jnp.concatenate([xh, xl], axis=0).T
    left_c[:, 384:400] = extras(self_term, 0, ROWS).T
    loads[2].wait()
    ph, pm, pl_ = split3(slab_probe_ref[...])
    left_p[:, 0:128] = jnp.concatenate([ph, pm, ph, pm], axis=0).T
    left_p[:, 128:192] = jnp.concatenate([ph, pl_], axis=0).T
    sh, sm, sl = split3(slab)
    left_s[...] = jnp.concatenate([sh, sm, sl, ones], axis=0)
    loads[3].wait()
    loads[4].wait()

    def compute(u, j, total):
        points = point_ref[:, columns(j, u)]
        probes = point_probe_ref[:, columns(j, u)]
        other_term = jnp.sum(w2 * points * points, axis=0, keepdims=True) * (-0.5 * LOG2E)
        yh, ym, yl = split3(points)
        right_c = jnp.concatenate([yh, ym, ym, yh, yl, yh, extras(other_term, 3, UNIT)], axis=0)
        gh, gm, gl = split3(probes)
        right_p = jnp.concatenate([gh, gm, gm, gh, gl, gh], axis=0)
        exponent = matmul(left_c[...], right_c, (1, 0))
        weights = jnp.exp2(exponent) * matmul(left_p[...], right_p, (1, 0))
        mh = weights.astype(BF16)
        ml = (weights - mh.astype(F32)).astype(BF16)
        ls = left_s[...]
        o2 = matmul(jnp.concatenate([ls, ls], axis=1), jnp.concatenate([mh, ml], axis=0), (1, 0))
        right_s = jnp.concatenate([yh, ym, yl, ones[:, :UNIT]], axis=0)
        o1 = matmul(jnp.concatenate([right_s, right_s], axis=1), jnp.concatenate([mh, ml], axis=1), (1, 1))
        mixed = o2[0:64] + o2[64:128] + o2[128:192]
        terms = w2 * (mixed - points * o2[192:193])
        for h in range(2):
            for v in range(2):
                part[u, j, h, v] = terms[h * HALF : h * HALF + HALF, v * 128 : v * 128 + 128]
        return o1 if total is None else total + o1

    def to_sibling(u, j):
        return go(part.at[u, j, other], sib_in.at[u, j], sibling)

    def take(c, u, j):
        c.wait_recv()
        part[u, j, core] = part[u, j, core] + sib_in[u, j]

    def far(u):
        a0 = go(part.at[u, 0, core, 0], r1.at[u, 0], z_down)
        a1 = go(part.at[u, 0, core, 1], r1.at[u, 1], z_up)
        return a0, a1

    def near(u):
        b1 = go(part.at[u, 1, core, 0], r2.at[u, 1, 0], z_up)
        b0 = go(part.at[u, 2, core, 1], r2.at[u, 0, 1], z_down)
        return b0, b1

    def near_sum(u, a):
        a[0].wait_recv()
        part[u, 2, core, 0] = part[u, 2, core, 0] + r1[u, 0]
        b2 = go(part.at[u, 2, core, 0], r2.at[u, 0, 0], z_down)
        a[1].wait_recv()
        part[u, 1, core, 1] = part[u, 1, core, 1] + r1[u, 1]
        b3 = go(part.at[u, 1, core, 1], r2.at[u, 1, 1], z_up)
        return b2, b3

    def share(u, piece, device, v=None):
        block = full.at[u, piece, core] if v is None else full.at[u, piece, core, v]
        return go(block, block, device)

    def finish(u, b, c):
        b[1].wait_recv()
        c[0].wait_recv()
        full[u, q, core, 0] = part[u, 3, core, 0] + r2[u, 0, 0] + r2[u, 1, 0]
        d0 = share(u, q, z_down, 0)
        b[0].wait_recv()
        c[1].wait_recv()
        full[u, q, core, 1] = part[u, 3, core, 1] + r2[u, 0, 1] + r2[u, 1, 1]
        d1 = share(u, q, z_up, 1)
        return d0, d1

    def finish_rest(u, d):
        d2 = share(u, q, z_up, 0)
        d3 = share(u, q, z_down, 1)
        return d + (d2, d3), [share(u, q, sibling)]

    def forward(u, d):
        d[0].wait_recv()
        f0 = share(u, p_up, z_down, 0)
        d[1].wait_recv()
        f1 = share(u, p_down, z_up, 1)
        return f0, f1

    def spread(u, d, e):
        d[2].wait_recv()
        e.append(share(u, p_down, sibling))
        d[3].wait_recv()
        e.append(share(u, p_up, sibling))

    def spread_far(u, f, e):
        f[0].wait_recv()
        e.append(share(u, p_far, sibling, 0))
        f[1].wait_recv()
        e.append(share(u, p_far, sibling, 1))

    def store(u, piece):
        for h in range(2):
            for v in range(2):
                lo = pl.multiple_of(piece * PIECE + u * UNIT + v * 128, 128)
                point_out[h * HALF : h * HALF + HALF, pl.ds(lo, 128)] = full[u, piece, h, v]

    total = compute(0, 0, None)
    pl.semaphore_wait(barrier, len(partners))
    s00 = to_sibling(0, 0)
    total = compute(1, 0, total)
    s10 = to_sibling(1, 0)
    total = compute(0, 1, total)
    s01 = to_sibling(0, 1)
    take(s00, 0, 0)
    a_0 = far(0)
    total = compute(0, 2, total)
    s02 = to_sibling(0, 2)
    take(s10, 1, 0)
    a_1 = far(1)
    total = compute(1, 1, total)
    s11 = to_sibling(1, 1)
    take(s01, 0, 1)
    total = compute(1, 2, total)
    s12 = to_sibling(1, 2)
    take(s02, 0, 2)
    b_0 = near(0)
    total = compute(0, 3, total)
    s03 = to_sibling(0, 3)
    take(s11, 1, 1)
    total = compute(1, 3, total)
    s13 = to_sibling(1, 3)
    take(s12, 1, 2)
    b_1 = near(1)

    slab_mixed = total[0:64] + total[64:128] + total[128:192]
    slab_terms = w2 * (slab_mixed - slab * total[192:193])
    for i in range(4):
        for k in range(4):
            sp[i, k] = slab_terms[16 * i : 16 * i + 16, 128 * k : 128 * k + 128]
    across = [go(sp.at[lax.rem(x + k, 4)], sx_in.at[k - 1], in_plane(k, 0)) for k in (1, 2, 3)]
    c_0 = near_sum(0, a_0)
    c_1 = near_sum(1, a_1)
    take(s03, 0, 3)
    take(s13, 1, 3)
    for c in across:
        c.wait_recv()
    sx[...] = sp[x] + sx_in[0] + sx_in[1] + sx_in[2]
    across = [go(sx.at[lax.rem(y + k, 4)], sy_in.at[k - 1], in_plane(0, k)) for k in (1, 2, 3)]

    for c in across:
        c.wait_recv()
    sz[zl] = sx[y] + sy_in[0] + sy_in[1] + sy_in[2]
    along = [go(sz.at[zl], sz.at[zl], at_l(k)) for k in (1, 2, 3)]

    d_0 = finish(0, b_0, c_0)
    d_1 = finish(1, b_1, c_1)
    d_0, e_0 = finish_rest(0, d_0)
    d_1, e_1 = finish_rest(1, d_1)
    for c in along:
        c.wait_recv()
    sf[x, y] = sz[0] + sz[1] + sz[2] + sz[3]
    gather = [go(sf.at[x, y], sf.at[x, y], in_plane(0, k)) for k in (1, 2, 3)]
    f_0 = forward(0, d_0)
    f_1 = forward(1, d_1)
    for c in gather:
        c.wait_recv()
    gather = [go(sf.at[x], sf.at[x], in_plane(k, 0)) for k in (1, 2, 3)]
    spread(0, d_0, e_0)
    spread(1, d_1, e_1)
    for u, e in enumerate((e_0, e_1)):
        for c in e:
            c.wait_recv()
        for j in (1, 2, 3):
            store(u, pieces[j])
    spread_far(0, f_0, e_0)
    spread_far(1, f_1, e_1)
    for c in gather:
        c.wait_recv()
    for i in range(4):
        for k in range(4):
            slab_out[16 * i : 16 * i + 16, 128 * k : 128 * k + 128] = sf[i, k]
    for u, e in enumerate((e_0, e_1)):
        for c in e[3:]:
            c.wait_recv()
        store(u, p_far)
    for c in sent:
        c.wait_send()


def local(slab_embed, slab_probe, point_embed, point_probe, inv_scale):
    vmem = pl.BlockSpec(memory_space=pltpu.VMEM)
    hbm = pl.BlockSpec(memory_space=pltpu.HBM)
    shapes = (
        jax.ShapeDtypeStruct(slab_embed.shape, F32),
        jax.ShapeDtypeStruct(point_embed.shape, F32),
    )
    operands = (inv_scale.reshape(1, EMB), slab_embed, slab_probe, point_embed, point_probe)
    return pl.pallas_call(
        kernel,
        name="pathwise_grad",
        out_shape=shapes,
        in_specs=[hbm] * 5,
        out_specs=(vmem, vmem),
        scratch_shapes=[
            pltpu.VMEM((1, EMB), F32),
            pltpu.VMEM(slab_embed.shape, F32),
            pltpu.VMEM(slab_probe.shape, F32),
            pltpu.VMEM(point_embed.shape, F32),
            pltpu.VMEM(point_probe.shape, F32),
            pltpu.VMEM((ROWS, 6 * EMB + 16), BF16),
            pltpu.VMEM((ROWS, 6 * PROBES), BF16),
            pltpu.VMEM((3 * EMB + 16, ROWS), BF16),
            pltpu.VMEM((2, 4, 2, 2, HALF, 128), F32),
            pltpu.VMEM((2, 4, 2, HALF, 128), F32),
            pltpu.VMEM((2, 2, HALF, 128), F32),
            pltpu.VMEM((2, 2, 2, HALF, 128), F32),
            pltpu.VMEM((2, 4, 2, 2, HALF, 128), F32),
            pltpu.VMEM((4, 4, 16, 128), F32),
            pltpu.VMEM((3, 4, 16, 128), F32),
            pltpu.VMEM((4, 16, 128), F32),
            pltpu.VMEM((3, 16, 128), F32),
            pltpu.VMEM((4, 16, 128), F32),
            pltpu.VMEM((4, 4, 16, 128), F32),
            pltpu.SemaphoreType.DMA((5,)),
            pltpu.SemaphoreType.DMA((80,)),
            pltpu.SemaphoreType.DMA((80,)),
        ],
        compiler_params=pltpu.CompilerParams(
            collective_id=0, has_side_effects=True, vmem_limit_bytes=VMEM_MIB * 1024 * 1024
        ),
    )(*(pltpu.with_memory_space_constraint(v, pltpu.HBM) for v in operands))


def solution(mesh):
    placed = (P(None, "row"), P(None, "row"), P(None, "col"), P(None, "col"), P())
    return jax.shard_map(
        local,
        mesh=mesh,
        in_specs=placed,
        out_specs=(P(None, "row"), P(None, "col")),
        check_vma=False,
    )
```

time: 783 us -> 45.7 us (0.06)
  waiting for transfers between devices: 743 us -> 0 us
  Pallas kernels: 0 us -> 43.5 us
  matrix products: 17.5 us -> 0 us
  between operations: 14.1 us -> 0.64 us
    psum x2 -> x0, waiting for transfers between devices: 742 us -> none  [the longest x1 623 us: local(): slab_grad = lax.psum(slab_terms, 'col')]
    pallas_call x0 -> x1, Pallas kernels: none -> 43.5 us  [local(): pl.pallas_call(kernel, name='pathwise_grad', out_shape=shapes, in_specs=[...]
    dot_general x8 -> x0, matrix products: 17.5 us -> none  [the longest x2 4.97 us: local(): mixed = mixed + jnp.dot(points, weights.T, precision=hp)]
  transfers between devices with their start and end apart: 2 -> 0, of which waited for: 2 -> 0; matrix products, arithmetic and copies ran while one was open for 0% -> 0% of each run, Pallas kernels for 0% -> 0%
where the time goes in v2:
time: 45.7 us; the launch traced here: 45.6 us
  Pallas kernels  43.5 us (95%)
  local copies, waits for them, and re-layouts  1.45 us (3%)
  between operations  0.64 us (1%)
    pallas_call x1, Pallas kernels, local(): pl.pallas_call(kernel, name='pathwise_grad', out_shape=shapes, in_specs=[...  43.5 us
    unnamed x2, local copies, waits for them, and re-layouts  1.45 us

profile of v2, /device:TPU:1, one launch (start us, length us, event | category | flops | bytes accessed | tf_op | source)
XLA Modules:
  0.0 45.6 jit_solution(14387795603410038629)
XLA Ops:
  0.6 43.5 %pathwise_grad.1 = (f32[64,512]{1,0:T(8,128)S(1)}, f32[64,2048]{1,0:T(8,128)S(1)}) custom-call(f32[1,64]{1,0:T(1,128)} %bitcast.1, f32[64,512]{1,0:T(8,128)} %slab_hbm.1, f32[32,512]{1,0:T(8,128)} %slab_probe_hbm.1, f32[64,2048]{1,0:T(8,128)} %point_hbm.1, f32[32,2048]{1,0:T(8,128)} %point_probe_hbm.1), custom_call_target="tpu_custom_call" | custom-call | tf_op jit(solution)/shard_map/pathwise_grad/pallas_call | solution.py:335
  44.1 0.7 %copy.9 = f32[64,512]{1,0:T(8,128)} copy(f32[64,512]{1,0:T(8,128)S(1)} %get-tuple-element.4) | data formatting | bytes 262144
  44.8 0.8 %copy.10 = f32[64,2048]{1,0:T(8,128)} copy(f32[64,2048]{1,0:T(8,128)S(1)} %get-tuple-element.5) | data formatting | bytes 1048576

commit v3 on v2

--- a/solution.py
+++ b/solution.py
@@ -284,24 +284,22 @@
     sx[...] = sp[x] + sx_in[0] + sx_in[1] + sx_in[2]
     across = [go(sx.at[lax.rem(y + k, 4)], sy_in.at[k - 1], in_plane(0, k)) for k in (1, 2, 3)]
 
-    for c in across:
-        c.wait_recv()
-    sz[zl] = sx[y] + sy_in[0] + sy_in[1] + sy_in[2]
-    along = [go(sz.at[zl], sz.at[zl], at_l(k)) for k in (1, 2, 3)]
 
     d_0 = finish(0, b_0, c_0)
     d_1 = finish(1, b_1, c_1)
     d_0, e_0 = finish_rest(0, d_0)
     d_1, e_1 = finish_rest(1, d_1)
+    for c in across:
+        c.wait_recv()
+    sz[zl] = sx[y] + sy_in[0] + sy_in[1] + sy_in[2]
+    along = [go(sz.at[zl], sz.at[zl], at_l(k)) for k in (1, 2, 3)]
+
     for c in along:
         c.wait_recv()
     sf[x, y] = sz[0] + sz[1] + sz[2] + sz[3]
-    gather = [go(sf.at[x, y], sf.at[x, y], in_plane(0, k)) for k in (1, 2, 3)]
+    gather = [go(sf.at[x, y], sf.at[x, y], in_plane(i, k)) for i in range(4) for k in range(4) if i or k]
     f_0 = forward(0, d_0)
     f_1 = forward(1, d_1)
-    for c in gather:
-        c.wait_recv()
-    gather = [go(sf.at[x], sf.at[x], in_plane(k, 0)) for k in (1, 2, 3)]
     spread(0, d_0, e_0)
     spread(1, d_1, e_1)
     for u, e in enumerate((e_0, e_1)):
@@ -324,6 +322,15 @@
         c.wait_send()
 
 
+def write_kernel(slab, point, slab_out, point_out, sems):
+    first = pltpu.make_async_copy(point, point_out, sems.at[0])
+    second = pltpu.make_async_copy(slab, slab_out, sems.at[1])
+    first.start()
+    second.start()
+    first.wait()
+    second.wait()
+
+
 def local(slab_embed, slab_probe, point_embed, point_probe, inv_scale):
     vmem = pl.BlockSpec(memory_space=pltpu.VMEM)
     hbm = pl.BlockSpec(memory_space=pltpu.HBM)
@@ -332,7 +339,7 @@
         jax.ShapeDtypeStruct(point_embed.shape, F32),
     )
     operands = (inv_scale.reshape(1, EMB), slab_embed, slab_probe, point_embed, point_probe)
-    return pl.pallas_call(
+    grads = pl.pallas_call(
         kernel,
         name="pathwise_grad",
         out_shape=shapes,
@@ -366,6 +373,14 @@
             collective_id=0, has_side_effects=True, vmem_limit_bytes=VMEM_MIB * 1024 * 1024
         ),
     )(*(pltpu.with_memory_space_constraint(v, pltpu.HBM) for v in operands))
+    return pl.pallas_call(
+        write_kernel,
+        name="write_out",
+        out_shape=shapes,
+        in_specs=[vmem] * 2,
+        out_specs=(hbm, hbm),
+        scratch_shapes=[pltpu.SemaphoreType.DMA((2,))],
+    )(*(pltpu.with_memory_space_constraint(v, pltpu.VMEM) for v in grads))
 
 
 def solution(mesh):

time: 45.7 us -> 43.8 us (0.958)
  local copies, waits for them, and re-layouts: 1.45 us -> 0 us
  Pallas kernels: 43.5 us -> 43 us
    unnamed x2 -> x0, local copies, waits for them, and re-layouts: 1.45 us -> none
    pallas_call x1, Pallas kernels: 43.5 us -> 42.1 us  [local(): pl.pallas_call(kernel, name='pathwise_grad', out_shape=shapes, in_specs=[...]
    pallas_call x0 -> x1, Pallas kernels: none -> 0.85 us  [local(): pl.pallas_call(write_kernel, name='write_out', out_shape=shapes, in_specs...]
where the time goes in v3:
time: 43.8 us; the launch traced here: 43.6 us
  Pallas kernels  43 us (98%)
  between operations  0.64 us (1%)
    pallas_call x1, Pallas kernels, local(): pl.pallas_call(kernel, name='pathwise_grad', out_shape=shapes, in_specs=[...  42.1 us

profile of v3, /device:TPU:1, one launch (start us, length us, event | category | flops | bytes accessed | tf_op | source)
XLA Modules:
  0.0 43.6 jit_solution(16658252574555360352)
XLA Ops:
  0.6 42.1 %pathwise_grad.1 = (f32[64,512]{1,0:T(8,128)S(1)}, f32[64,2048]{1,0:T(8,128)S(1)}) custom-call(f32[1,64]{1,0:T(1,128)} %bitcast.1, f32[64,512]{1,0:T(8,128)} %slab_hbm.1, f32[32,512]{1,0:T(8,128)} %slab_probe_hbm.1, f32[64,2048]{1,0:T(8,128)} %point_hbm.1, f32[32,2048]{1,0:T(8,128)} %point_probe_hbm.1), custom_call_target="tpu_custom_call" | custom-call | tf_op jit(solution)/shard_map/pathwise_grad/pallas_call | solution.py:342
  42.8 0.8 %write_out.1 = (f32[64,512]{1,0:T(8,128)}, f32[64,2048]{1,0:T(8,128)}) custom-call(f32[64,512]{1,0:T(8,128)S(1)} %get-tuple-element.4.slab, f32[64,2048]{1,0:T(8,128)S(1)} %get-tuple-element.5.point), custom_call_target="tpu_custom_call" | custom-call | tf_op jit(solution)/shard_map/write_out/pallas_call | solution.py:376

commit v4 on v3

--- a/solution.py
+++ b/solution.py
@@ -309,15 +309,15 @@
             store(u, pieces[j])
     spread_far(0, f_0, e_0)
     spread_far(1, f_1, e_1)
-    for c in gather:
-        c.wait_recv()
-    for i in range(4):
-        for k in range(4):
-            slab_out[16 * i : 16 * i + 16, 128 * k : 128 * k + 128] = sf[i, k]
     for u, e in enumerate((e_0, e_1)):
         for c in e[3:]:
             c.wait_recv()
         store(u, p_far)
+    for c in gather:
+        c.wait_recv()
+    for i in range(4):
+        for k in range(4):
+            slab_out[16 * i : 16 * i + 16, 128 * k : 128 * k + 128] = sf[i, k]
     for c in sent:
         c.wait_send()
 

time: 43.8 us -> 43.8 us (level)
  no operation moved by 1% of the time
where the time goes in v4:
time: 43.8 us; the launch traced here: 43.7 us
  Pallas kernels  43 us (98%)
  between operations  0.64 us (1%)
    pallas_call x1, Pallas kernels, local(): pl.pallas_call(kernel, name='pathwise_grad', out_shape=shapes, in_specs=[...  42.2 us

profile of v4, /device:TPU:1, one launch (start us, length us, event | category | flops | bytes accessed | tf_op | source)
XLA Modules:
  0.0 43.7 jit_solution(6405111891755955331)
XLA Ops:
  0.6 42.2 %pathwise_grad.1 = (f32[64,512]{1,0:T(8,128)S(1)}, f32[64,2048]{1,0:T(8,128)S(1)}) custom-call(f32[1,64]{1,0:T(1,128)} %bitcast.1, f32[64,512]{1,0:T(8,128)} %slab_hbm.1, f32[32,512]{1,0:T(8,128)} %slab_probe_hbm.1, f32[64,2048]{1,0:T(8,128)} %point_hbm.1, f32[32,2048]{1,0:T(8,128)} %point_probe_hbm.1), custom_call_target="tpu_custom_call" | custom-call | tf_op jit(solution)/shard_map/pathwise_grad/pallas_call | solution.py:342
  42.8 0.8 %write_out.1 = (f32[64,512]{1,0:T(8,128)}, f32[64,2048]{1,0:T(8,128)}) custom-call(f32[64,512]{1,0:T(8,128)S(1)} %get-tuple-element.4.slab, f32[64,2048]{1,0:T(8,128)S(1)} %get-tuple-element.5.point), custom_call_target="tpu_custom_call" | custom-call | tf_op jit(solution)/shard_map/write_out/pallas_call | solution.py:376
